TPU v7x, 32 devices: a whole 2x2x4 slice. The times are simulated.
32 devices in a mesh: ctx: 8 (over y, x, core), head: 4 (over z).
Axes of the slice: x: 2, y: 2, z: 4, core: 2. Of those that a mesh axis runs over, the one named last changes fastest.
Arguments:
- branch_rows: bfloat16 [4096, 2048], P(('ctx', 'head')), may hold values from -6 to 6
- expert_ids: int32 [4096, 8], P(('ctx', 'head')), may hold values from 0 to 31, all different within a row; in each aligned block of 128 rows (0 to 127, 128 to 255, ...) at most 48 rows name the same one
- targets: int32 [4096], P(('ctx', 'head')), may hold values from 0 to 4095, as said below
- router: bfloat16 [2048, 32], replicated, may hold values from -0.046875 to 0.046875
- w_gate: bfloat16 [32, 2048, 768], P(('ctx', 'head')), may hold values from -0.125 to 0.125
- w_up: bfloat16 [32, 2048, 768], P(('ctx', 'head')), may hold values from -0.125 to 0.125
- w_down: bfloat16 [32, 768, 2048], P(('ctx', 'head')), may hold values from -0.3125 to 0.3125
- stream: bfloat16 [4096, 2048], P('ctx', 'head'), may hold values from -6 to 6
- attn_gain: float32 [2048], replicated, may hold values from 0.1 to 1.9
- q_gain: float32 [4096], P('head'), may hold values from 0.5 to 7
- k_gain: float32 [512], replicated, may hold values from 0.8 to 6
- w_query: bfloat16 [2048, 4096], P(None, 'head')
- w_key: bfloat16 [2048, 512], replicated
- w_value: bfloat16 [2048, 512], replicated, may hold values from -0.125 to 0.125
- w_out: bfloat16 [4096, 2048], P('head'), may hold values from -0.375 to 0.375
Outputs:
- layer_out: bfloat16 [4096, 2048], P('ctx', 'head')
Inputs may be any that keep to these rules, and one draw needn't show every extreme that they name: `expert_ids`: in each device's 128 rows no expert is named more than 48 times. `targets`: each device's 128 rows name exactly 16 positions in each block of 512 joined positions; positions may repeat.
All inputs are finite; a program needn't handle non-finite values.
Results may differ from a plain program's by a relative error of at most 0.018.
Values may be sent and summed in bfloat16 or wider, within the bound.
A program may use at most 192 MiB of HBM per device.

v0:
```python
import functools
import math

import jax
import jax.numpy as jnp
from jax import lax
from jax.experimental import pallas as pl
from jax.experimental.pallas import tpu as pltpu
from jax.sharding import PartitionSpec as P

QH = 32
KVH = 4
HD = 128

EPSILON = 1e-06
THETA = 1000000.0
BOTH = ("ctx", "head")


def rotary_tables(positions):
    half_dim = HD // 2
    frequency = jnp.power(
        jnp.float32(THETA), -jnp.arange(half_dim, dtype=jnp.float32) * 2.0 / HD
    )
    angles = positions.astype(jnp.float32)[:, None] * frequency[None, :]
    cosines = jnp.cos(angles)
    sines = jnp.sin(angles)
    return jnp.concatenate([cosines, cosines], -1), jnp.concatenate([-sines, sines], -1)


def exclusive_count(onehot):
    rows = onehot.shape[-2]
    lower = (jnp.arange(rows)[:, None] > jnp.arange(rows)[None, :]).astype(jnp.bfloat16)
    return jnp.einsum("rq,...qe->...re", lower, onehot, preferred_element_type=jnp.float32)


def pick_kernel(pick_ref, rows_ref, out_ref):
    for i in range(pick_ref.shape[0]):
        out_ref[i] = jnp.dot(
            pick_ref[i], rows_ref[i], preferred_element_type=jnp.float32
        ).astype(out_ref.dtype)


def pick_rows(pick, gathered, width):
    blocks, capacity, rows = pick.shape
    group = 4
    return pl.pallas_call(
        pick_kernel,
        grid=(blocks // group,),
        in_specs=[
            pl.BlockSpec((group, capacity, rows), lambda b: (b, 0, 0)),
            pl.BlockSpec((group, rows, width), lambda b: (b, 0, 0)),
        ],
        out_specs=pl.BlockSpec((group, capacity, width), lambda b: (b, 0, 0)),
        out_shape=jax.ShapeDtypeStruct((blocks, capacity, width), jnp.bfloat16),
        name="pick_rows",
    )(pick, gathered)


def spread_kernel(per_owner, pick_ref, rows_ref, out_ref):
    owners = out_ref.shape[0]
    width = rows_ref.shape[2]
    for i in range(pick_ref.shape[0]):
        spread = jnp.dot(pick_ref[i], rows_ref[i], preferred_element_type=jnp.float32)
        out_ref[:, i] = spread.astype(out_ref.dtype).reshape(owners, per_owner, width)


def spread_rows(pick, weighted, owners):
    blocks, rows, capacity = pick.shape
    width = weighted.shape[2]
    per_owner = rows // owners
    group = 4
    return pl.pallas_call(
        functools.partial(spread_kernel, per_owner),
        grid=(blocks // group,),
        in_specs=[
            pl.BlockSpec((group, rows, capacity), lambda b: (b, 0, 0)),
            pl.BlockSpec((group, capacity, width), lambda b: (b, 0, 0)),
        ],
        out_specs=pl.BlockSpec((owners, group, per_owner, width), lambda b: (0, b, 0, 0)),
        out_shape=jax.ShapeDtypeStruct((owners, blocks, per_owner, width), jnp.bfloat16),
        name="spread_rows",
    )(pick, weighted)


def attention_kernel(pair, tokens, first_row, q_ref, cos_ref, sin_ref, gain_ref, kv_ref, out_ref, m_ref, a_ref):
    rows_here = q_ref.shape[0]
    here = lax.axis_index("ctx")
    factor = math.log2(math.e) / math.sqrt(HD)
    heads = []
    for i in range(pair):
        lanes = slice(i * HD, (i + 1) * HD)
        raw = q_ref[:, lanes]
        scaled = raw * lax.rsqrt(jnp.mean(raw * raw, -1, keepdims=True) + EPSILON)
        scaled = scaled * (gain_ref[:, lanes] * factor)
        turned = scaled * cos_ref[...] + pltpu.roll(scaled, HD // 2, 1) * sin_ref[...]
        heads.append(turned.astype(jnp.bfloat16))

    def piece(start, length, masked, first):
        keys = kv_ref[pl.ds(start, length), :HD]
        values = kv_ref[pl.ds(start, length), HD:]
        values = jnp.concatenate([values, jnp.ones_like(values)], 1)
        if masked:
            rows = lax.broadcasted_iota(jnp.int32, (rows_here, length), 0) + first_row
            cols = lax.broadcasted_iota(jnp.int32, (rows_here, length), 1)
        for i in range(pair):
            lanes = slice(i * HD, (i + 1) * HD)
            wide = slice(i * 2 * HD, (i + 1) * 2 * HD)
            scores = lax.dot_general(
                heads[i], keys, (((1,), (1,)), ((), ())), preferred_element_type=jnp.float32
            )
            if masked:
                scores = jnp.where(rows >= cols, scores, -1e30)
            top = jnp.max(scores, -1, keepdims=True)
            if first:
                fresh = jnp.broadcast_to(top, (rows_here, HD))
            else:
                old = m_ref[:, lanes]
                fresh = jnp.maximum(old, top)
            weights = jnp.exp2(scores - fresh[:, :1]).astype(jnp.bfloat16)
            part = jnp.dot(weights, values, preferred_element_type=jnp.float32)
            if first:
                a_ref[:, wide] = part
            else:
                decay = jnp.exp2(old - fresh)
                a_ref[:, wide] = a_ref[:, wide] * jnp.concatenate([decay, decay], 1) + part
            m_ref[:, lanes] = fresh

    piece(pl.multiple_of(here * tokens, tokens), first_row + rows_here, True, True)

    def step(j, carry):
        piece(pl.multiple_of(j * tokens, tokens), tokens, False, False)
        return carry

    lax.fori_loop(0, here, step, 0)
    for i in range(pair):
        begin = i * 2 * HD
        out_ref[:, i * HD : (i + 1) * HD] = (
            a_ref[:, begin : begin + HD] / a_ref[:, begin + HD : begin + 2 * HD]
        ).astype(out_ref.dtype)


def attention(queries, cos, sin, gain, kv, part, parts):
    tokens, width = queries.shape
    rows = tokens // parts
    pair = 4
    cols = pair * HD
    work = rows * kv.shape[0] * width
    return pl.pallas_call(
        functools.partial(attention_kernel, pair, tokens, part * rows),
        grid=(width // cols,),
        in_specs=[
            pl.BlockSpec((rows, cols), lambda i: (part, i)),
            pl.BlockSpec((rows, HD), lambda i: (part, 0)),
            pl.BlockSpec((rows, HD), lambda i: (part, 0)),
            pl.BlockSpec((1, cols), lambda i: (0, i)),
            pl.BlockSpec(kv.shape, lambda i: (0, 0)),
        ],
        out_specs=pl.BlockSpec((rows, cols), lambda i: (0, i)),
        out_shape=jax.ShapeDtypeStruct((rows, width), jnp.bfloat16),
        scratch_shapes=[
            pltpu.VMEM((rows, cols), jnp.float32),
            pltpu.VMEM((rows, 2 * cols), jnp.float32),
        ],
        cost_estimate=pl.CostEstimate(
            flops=8 * work, bytes_accessed=4 * rows * width * 2, transcendentals=work // HD
        ),
        name=f"attention_{part}",
    )(queries, cos, sin, gain, kv)


def body(
    branch_rows,
    expert_ids,
    targets,
    router,
    w_gate,
    w_up,
    w_down,
    stream,
    attn_gain,
    q_gain,
    k_gain,
    w_query,
    w_key,
    w_value,
    w_out,
):
    ctx_count = lax.axis_size("ctx")
    head_count = lax.axis_size("head")
    devices = ctx_count * head_count
    experts = router.shape[1]
    rows_here = branch_rows.shape[0]
    top_count = expert_ids.shape[1]
    model_width = branch_rows.shape[1]
    capacity = 3 * rows_here * top_count // (2 * experts)
    local_tokens = stream.shape[0]
    per_owner = rows_here // ctx_count
    ctx_here = lax.axis_index("ctx")
    head_here = lax.axis_index("head")

    owner_ids = targets // local_tokens
    owned = owner_ids[:, None] == jnp.arange(ctx_count, dtype=jnp.int32)[None, :]
    order_in = jnp.sum(
        jnp.where(owned, exclusive_count(owned.astype(jnp.bfloat16)), 0.0), 1
    ).astype(jnp.int32)
    place = owner_ids * per_owner + order_in
    turn = place[None, :] == jnp.arange(rows_here, dtype=jnp.int32)[:, None]
    turn_bf = turn.astype(jnp.bfloat16)
    ordered = jnp.dot(turn_bf, branch_rows, preferred_element_type=jnp.float32).astype(jnp.bfloat16)
    ids = jnp.dot(
        turn_bf, expert_ids.astype(jnp.bfloat16), preferred_element_type=jnp.float32
    ).astype(jnp.int32)
    spots = jnp.sum(jnp.where(turn, (targets % local_tokens)[None, :], 0), 1)
    logits = jnp.dot(ordered, router, preferred_element_type=jnp.float32)
    chosen = jnp.any(
        ids[:, :, None] == jnp.arange(experts, dtype=jnp.int32)[None, None, :], axis=1
    )
    highest = jnp.max(jnp.where(chosen, logits, -jnp.inf), -1, keepdims=True)
    raised = jnp.where(chosen, jnp.exp(jnp.where(chosen, logits - highest, 0.0)), 0.0)
    gates = raised / jnp.sum(raised, -1, keepdims=True)
    gates_high = lax.reduce_precision(gates, 8, 7)
    gates_low = gates - gates_high
    spots_high = (spots // 128).astype(jnp.float32)[:, None]
    spots_low = (spots % 128).astype(jnp.float32)[:, None]
    extra = jnp.concatenate([gates_high, gates_low, spots_high, spots_low], 1).astype(jnp.bfloat16)
    extra_width = -(-extra.shape[1] // 128) * 128
    extra = jnp.pad(extra, ((0, 0), (0, extra_width - extra.shape[1])))
    gathered = lax.all_gather(
        jnp.concatenate([ordered, extra], 1), BOTH, axis=0, tiled=True
    )

    mine = ctx_here * head_count + head_here
    notes = gathered[:, model_width:].astype(jnp.float32)
    column = jnp.arange(extra_width, dtype=jnp.int32)
    my_gate = jnp.sum(
        jnp.where((column == mine) | (column == experts + mine), notes, 0.0), 1
    ).reshape(devices, rows_here)
    wanted = my_gate > 0.0
    rank = exclusive_count(wanted.astype(jnp.bfloat16)[:, :, None])[:, :, 0].astype(jnp.int32)
    pick = (
        (rank[:, None, :] == jnp.arange(capacity, dtype=jnp.int32)[None, :, None])
        & wanted[:, None, :]
    )
    slot_gate = jnp.sum(jnp.where(pick, my_gate[:, None, :], 0.0), -1)
    pick_bf = pick.astype(jnp.bfloat16)
    back_bf = (
        (rank[:, :, None] == jnp.arange(capacity, dtype=jnp.int32)[None, None, :])
        & wanted[:, :, None]
    ).astype(jnp.bfloat16)
    inputs = pick_rows(
        pick_bf, gathered.reshape(devices, rows_here, -1), model_width
    ).reshape(devices * capacity, model_width)
    gate_part = jnp.dot(inputs, w_gate[0], preferred_element_type=jnp.float32)
    upward = jnp.dot(inputs, w_up[0], preferred_element_type=jnp.float32)
    hidden = (jax.nn.silu(gate_part) * upward).astype(jnp.bfloat16)
    produced = jnp.dot(hidden, w_down[0], preferred_element_type=jnp.float32)
    weighted = (produced * slot_gate.reshape(-1, 1)).astype(jnp.bfloat16)
    shares = spread_rows(
        back_bf, weighted.reshape(devices, capacity, model_width), ctx_count
    ).reshape(devices * rows_here, model_width)
    landed = lax.psum_scatter(shares, "ctx", scatter_dimension=0, tiled=True)
    landed = lax.psum_scatter(landed, "head", scatter_dimension=1, tiled=True)

    notes4 = notes.reshape(devices, ctx_count, per_owner, extra_width)
    notes_here = lax.dynamic_index_in_dim(notes4, ctx_here, 1, keepdims=False)
    spot_ids = (
        notes_here[:, :, 2 * experts] * 128.0 + notes_here[:, :, 2 * experts + 1]
    ).astype(jnp.int32).reshape(-1)
    aimed = (
        jnp.arange(local_tokens, dtype=jnp.int32)[:, None] == spot_ids[None, :]
    ).astype(jnp.bfloat16)
    joined = (
        stream.astype(jnp.float32) + jnp.dot(aimed, landed, preferred_element_type=jnp.float32)
    ).astype(jnp.bfloat16)
    full_rows = lax.all_gather(joined, "head", axis=1, tiled=True)
    full_float = full_rows.astype(jnp.float32)
    normed = (
        full_float
        * lax.rsqrt(jnp.mean(full_float * full_float, -1, keepdims=True) + EPSILON)
        * attn_gain
    ).astype(jnp.bfloat16)
    per_device = w_query.shape[1] // HD
    kv_head = head_here * per_device // (QH // KVH)
    positions = ctx_here * local_tokens + jnp.arange(local_tokens, dtype=jnp.int32)
    cos, sin = rotary_tables(positions)
    key_value = jnp.concatenate(
        [
            lax.dynamic_slice_in_dim(w_key, kv_head * HD, HD, 1),
            lax.dynamic_slice_in_dim(w_value, kv_head * HD, HD, 1),
        ],
        1,
    )
    key_scales = lax.dynamic_slice_in_dim(k_gain, kv_head * HD, HD, 0)
    kv_rows = jnp.dot(normed, key_value, preferred_element_type=jnp.float32)
    keys = kv_rows[:, :HD]
    keys = keys * lax.rsqrt(jnp.mean(keys * keys, -1, keepdims=True) + EPSILON) * key_scales
    keys = keys * cos + jnp.roll(keys, HD // 2, 1) * sin
    kv = lax.all_gather(
        jnp.concatenate([keys, kv_rows[:, HD:]], 1).astype(jnp.bfloat16), "ctx", axis=0, tiled=True
    )
    queries = jnp.dot(normed, w_query, preferred_element_type=jnp.float32)
    parts = 2
    rows_part = local_tokens // parts
    sums = []
    for part in range(parts):
        attended = attention(queries, cos, sin, q_gain.reshape(1, -1), kv, part, parts)
        partial_out = jnp.dot(attended, w_out, preferred_element_type=jnp.float32)
        summed = lax.psum_scatter(
            partial_out.astype(jnp.bfloat16), "head", scatter_dimension=1, tiled=True
        )
        sums.append(
            joined[part * rows_part : (part + 1) * rows_part].astype(jnp.float32)
            + summed.astype(jnp.float32)
        )
    return jnp.concatenate(sums, 0).astype(jnp.bfloat16)


def solution(mesh):
    in_specs = (
        P(("ctx", "head"), None),
        P(("ctx", "head"), None),
        P(("ctx", "head")),
        P(),
        P(("ctx", "head"), None, None),
        P(("ctx", "head"), None, None),
        P(("ctx", "head"), None, None),
        P("ctx", "head"),
        P(),
        P("head"),
        P(),
        P(None, "head"),
        P(),
        P(),
        P("head", None),
    )
    out_specs = P("ctx", "head")
    return jax.shard_map(body, mesh=mesh, in_specs=in_specs, out_specs=out_specs, check_vma=False)
```

profile of v0, /device:TPU:7, one launch (start us, length us, event | category | flops | bytes accessed | tf_op | source)
XLA Modules:
  0.0 522.7 jit_solution(1074454392256965593)
XLA Ops:
  6.5 0.8 and_select_fusion.3
  7.4 0.1 fusion.11
  7.5 0.1 select_reduce_fusion.2
  7.7 0.8 convolution_convert_fusion.4
  8.5 1.3 convolution_convert_fusion.2
  9.9 0.8 copy-done.3
  10.7 1.2 select_reduce_fusion.3
  12.0 0.1 copy.50
  12.1 1.9 fusion.21
  14.1 119.8 %all-gather.4.cloned.1.call-done = bf16[4096,2176]{1,0:T(8,128)(2,1)} async-done(((bf16[128,2176]{1,0:T(8,128)(2,1)}), bf16[4096,2176]{1,0:T(8,128)(2,1)}) %all-gather.4.cloned.1.call-update) | async-done | bytes 17825808 | tf_op jit(solution)/shard_map/all_gather | solution.py:229
  133.9 1.6 select_reduce_fusion
  135.5 0.1 convolution_convert_fusion.3
  135.7 0.9 fusion.17.pick_ref
  136.6 2.4 fusion.8.pick_ref
  139.0 0.3 select_reduce_fusion.1
  139.3 0.1 mul.115
  139.4 11.6 %pick_rows.1 = bf16[32,48,2048]{2,1,0:T(8,128)(2,1)} custom-call(bf16[32,48,128]{2,1,0:T(8,128)(2,1)} %fusion.17.pick_ref, bf16[32,128,2176]{2,1,0:T(8,128)(2,1)} %bitcast.51), custom_call_target="tpu_custom_call" | custom-call | tf_op jit(solution)/shard_map/pick_rows/pallas_call | solution.py:47
  151.0 8.2 %fusion.5 = f32[1536,768]{1,0:T(8,128)S(1)} fusion(bf16[1536,2048]{1,0:T(8,128)(2,1)} %bitcast.53, bf16[1,2048,768]{2,1,0:T(8,128)(2,1)} %param.19), kind=kOutput, calls=%fused_computation.9 | convolution fusion | flops 4831838208 | bytes 14155776 | tf_op jit(solution)/shard_map/dot_general | solution.py:254
  159.2 5.6 %multiply_convert_fusion.1 = bf16[1536,768]{1,0:T(8,128)(2,1)S(1)} fusion(f32[1536,768]{1,0:T(8,128)S(1)} %fusion.5, bf16[1536,2048]{1,0:T(8,128)(2,1)S(1)} %bitcast.54, bf16[1,2048,768]{2,1,0:T(8,128)(2,1)S(1)} %copy-done.6), kind=kOutput, calls=%fused_computation.3 | convolution fusion | flops 4838916096 | bytes 16515072 | tf_op jit(solution)/shard_map/dot_general | solution.py:255
  164.9 7.1 %multiply_convert_fusion = bf16[1536,2048]{1,0:T(8,128)(2,1)} fusion(bf16[1536,768]{1,0:T(8,128)(2,1)S(1)} %multiply_convert_fusion.1, f32[1536]{0:T(1024)S(1)} %mul.115, bf16[1,768,2048]{2,1,0:T(8,128)(2,1)S(1)} %copy-done), kind=kOutput, calls=%fused_computation | convolution fusion | flops 4838129664 | bytes 11802624 | tf_op jit(solution)/shard_map/dot_general | solution.py:257
  172.0 12.3 %spread_rows.1 = bf16[8,32,16,2048]{3,2,1,0:T(8,128)(2,1)} custom-call(bf16[32,128,48]{2,1,0:T(8,128)(2,1)} %fusion.8.pick_ref, bf16[32,48,2048]{2,1,0:T(8,128)(2,1)} %bitcast.52), custom_call_target="tpu_custom_call" | custom-call | tf_op jit(solution)/shard_map/spread_rows/pallas_call | solution.py:73
  184.3 113.9 %reduce-scatter.5.cloned.1.call-done = bf16[512,2048]{1,0:T(8,128)(2,1)} async-done(((bf16[4096,2048]{1,0:T(8,128)(2,1)}), bf16[512,2048]{1,0:T(8,128)(2,1)}) %reduce-scatter.5.cloned.1.call-update) | async-done | bytes 2097168 | tf_op jit(solution)/shard_map/reduce_scatter | solution.py:262
  298.4 1.4 slice_convert_fusion
  299.8 1.8 copy.46
  301.7 0.1 convert_element_type.121
  301.7 43.2 %reduce-scatter.7.cloned.1.call-done = bf16[512,512]{1,0:T(8,128)(2,1)} async-done(((bf16[512,2048]{1,0:T(8,128)(2,1)}), bf16[512,512]{1,0:T(8,128)(2,1)}) %reduce-scatter.7.cloned.1.call-update) | async-done | bytes 524304 | tf_op jit(solution)/shard_map/reduce_scatter | solution.py:263
  344.9 2.3 fusion.9
  347.2 0.2 all-gather.8.cloned.1.call-start
  347.5 0.8 dynamic_slice.16
  348.3 1.8 fusion.26
  350.0 1.3 constant_dynamic-slice_fusion
  351.3 41.2 %all-gather.6.cloned.1.call-done = bf16[512,2048]{1,0:T(8,128)(2,1)} async-done(((bf16[512,512]{1,0:T(8,128)(2,1)}), bf16[512,2048]{1,0:T(8,128)(2,1)}) %all-gather.6.cloned.1.call-update) | async-done | bytes 2097168 | tf_op jit(solution)/shard_map/all_gather | solution.py:276
  392.5 2.1 fusion
  394.6 2.4 fusion.12
  397.0 0.1 multiply_reduce_fusion
  397.2 0.1 multiply_multiply_fusion
  397.3 0.1 fusion.38
  397.5 1.2 fusion.24
  398.6 0.7 pad_maximum_fusion.3
  399.5 5.9 %fusion.19.q_ref = f32[512,1024]{1,0:T(8,128)} fusion(bf16[2048,1024]{1,0:T(8,128)(2,1)} %param.26, bf16[512,2048]{1,0:T(8,128)(2,1)S(1)} %copy-done.4, f32[2048]{0:T(1024)S(1)} %copy-done.8, f32[512]{0:T(512)S(1)} %add_rsqrt_fusion.1), kind=kOutput, calls=%fused_computation.36 | convolution fusion | flops 2151677952 | bytes 8398848 | tf_op jit(solution)/shard_map/dot_general | solution.py:302
  405.3 20.4 %all-gather.8.cloned.1.call-done.kv_ref = bf16[4096,256]{1,0:T(8,128)(2,1)} async-done(((bf16[512,256]{1,0:T(8,128)(2,1)}), bf16[4096,256]{1,0:T(8,128)(2,1)}) %all-gather.8.cloned.1.call-update) | async-done | bytes 2097168 | tf_op jit(solution)/shard_map/all_gather | solution.py:299
  425.8 26.1 %attention_0.1 = bf16[256,1024]{1,0:T(8,128)(2,1)} custom-call(f32[512,1024]{1,0:T(8,128)} %fusion.19.q_ref, f32[512,128]{1,0:T(8,128)} %get-tuple-element.9.cos_ref, f32[512,128]{1,0:T(8,128)} %get-tuple-element.6.sin_ref, f32[1,1024]{1,0:T(1,128)} %bitcast.58, bf16[4096,256]{1,0:T(8,128)(2,1)} %all-gather.8.cloned.1.call-done.kv_ref), custom_call_target="tpu_custom_call" | custom-call | flops 8589934592 | bytes 2097152 | tf_op jit(solution)/shard_map/attention_0/pallas_call | solution.py:149
  451.8 4.6 convolution_convert_fusion.1
  456.4 0.0 reduce-scatter.11.cloned.1.call-start
  456.5 25.2 %attention_1.1 = bf16[256,1024]{1,0:T(8,128)(2,1)} custom-call(f32[512,1024]{1,0:T(8,128)} %fusion.19.q_ref, f32[512,128]{1,0:T(8,128)} %get-tuple-element.9.cos_ref, f32[512,128]{1,0:T(8,128)} %get-tuple-element.6.sin_ref, f32[1,1024]{1,0:T(1,128)} %bitcast.59, bf16[4096,256]{1,0:T(8,128)(2,1)} %all-gather.8.cloned.1.call-done.kv_ref), custom_call_target="tpu_custom_call" | custom-call | flops 8589934592 | bytes 2097152 | tf_op jit(solution)/shard_map/attention_1/pallas_call | solution.py:149
  481.7 4.6 convolution_convert_fusion
  486.4 27.4 %reduce-scatter.11.cloned.1.call-done = bf16[256,512]{1,0:T(8,128)(2,1)} async-done(((bf16[256,2048]{1,0:T(8,128)(2,1)}), bf16[256,512]{1,0:T(8,128)(2,1)}) %reduce-scatter.11.cloned.1.call-update) | async-done | bytes 262160 | tf_op jit(solution)/shard_map/reduce_scatter | solution.py:309
  513.8 2.1 add_convert_fusion.1
  (46 shorter events, 0.6 us)
Async XLA Ops:
  6.5 158.3 %copy-start = (bf16[1,768,2048]{2,1,0:T(8,128)(2,1)S(1)}, bf16[1,768,2048]{2,1,0:T(8,128)(2,1)}, u32[]{:S(2)}) copy-start(bf16[1,768,2048]{2,1,0:T(8,128)(2,1)} %param.21) | copy-start | bytes 9437188
  6.5 127.4 %all-gather.4.cloned.1.call-start = ((), (), s32[]{:S(2)}) async-start(), calls=%async_computation.4 | async-start | bytes 18382848 | tf_op jit(solution)/shard_map/all_gather | solution.py:229
  9.9 0.8 copy-start.3
  14.0 284.3 %reduce-scatter.5.cloned.1.call-start = ((), (), s32[]{:S(2)}) async-start(), calls=%async_computation.5 | async-start | bytes 18874368 | tf_op jit(solution)/shard_map/reduce_scatter | solution.py:262
  151.0 8.2 %copy-start.2 = (bf16[32,48,2048]{2,1,0:T(8,128)(2,1)S(1)}, bf16[32,48,2048]{2,1,0:T(8,128)(2,1)}, u32[]{:S(2)}) copy-start(bf16[32,48,2048]{2,1,0:T(8,128)(2,1)} %pick_rows.1) | copy-start | bytes 18874372
  151.0 8.2 %copy-start.6 = (bf16[1,2048,768]{2,1,0:T(8,128)(2,1)S(1)}, bf16[1,2048,768]{2,1,0:T(8,128)(2,1)}, u32[]{:S(2)}) copy-start(bf16[1,2048,768]{2,1,0:T(8,128)(2,1)} %param.20) | copy-start | bytes 9437188
  184.3 160.6 %reduce-scatter.7.cloned.1.call-start = ((), (), s32[]{:S(2)}) async-start(), calls=%async_computation.6 | async-start | bytes 2621440 | tf_op jit(solution)/shard_map/reduce_scatter | solution.py:263
  298.3 46.6 %copy-start.7 = (bf16[512,512]{1,0:T(8,128)(2,1)S(1)}, bf16[512,512]{1,0:T(8,128)(2,1)}, u32[]{:S(2)}) copy-start(bf16[512,512]{1,0:T(8,128)(2,1)} %param.22) | copy-start | bytes 1572868
  298.3 94.2 %all-gather.6.cloned.1.call-start = ((), (), s32[]{:S(2)}) async-start(), calls=%async_computation.7 | async-start | bytes 2621440 | tf_op jit(solution)/shard_map/all_gather | solution.py:276
  347.2 47.4 %copy-start.8 = (f32[2048]{0:T(1024)S(1)}, f32[2048]{0:T(1024)}, u32[]{:S(2)}) copy-start(f32[2048]{0:T(1024)} %param.23) | copy-start | bytes 24580
  347.2 78.5 %all-gather.8.cloned.1.call-start = ((), (), s32[]{:S(2)}) async-start(), calls=%async_computation.8 | async-start | bytes 2359296 | tf_op jit(solution)/shard_map/all_gather | solution.py:299
  394.6 2.9 copy-start.5
  397.0 2.5 copy-start.4
  399.4 87.0 %reduce-scatter.9.cloned.1.call-start = ((), (), s32[]{:S(2)}) async-start(), calls=%async_computation.9 | async-start | bytes 1310720 | tf_op jit(solution)/shard_map/reduce_scatter | solution.py:309
  456.4 57.3 %reduce-scatter.11.cloned.1.call-start = ((), (), s32[]{:S(2)}) async-start(), calls=%async_computation.10 | async-start | bytes 1310720 | tf_op jit(solution)/shard_map/reduce_scatter | solution.py:309
  456.5 59.4 %copy-start.1 = (bf16[1,768,2048]{2,1,0:T(8,128)(2,1)S(1)}, bf16[1,768,2048]{2,1,0:T(8,128)(2,1)}, u32[]{:S(2)}) copy-start(bf16[1,768,2048]{2,1,0:T(8,128)(2,1)} %param.21) | copy-start | bytes 9437188
Sparse Core Ops, SparseCore 0:
  14.1 119.7 all-gather.3
  184.4 113.8 reduce-scatter.4
  300.6 44.2 reduce-scatter.6
  347.4 45.0 all-gather.5
  399.5 26.2 all-gather.7
  456.6 26.9 reduce-scatter.8
  486.5 27.2 reduce-scatter.10
where the time goes:
time: 526 us; the launch traced here: 523 us
  waiting for transfers between devices  366 us (70%)
  Pallas kernels  75.2 us (14%)
  matrix products  44.3 us (8%)
  other arithmetic  17.8 us (3%)
  between operations  13.8 us (3%)
    all_gather x1, waiting for transfers between devices, body(): lax.all_gather(jnp.concatenate([ordered, extra], 1), BOTH, axis=0, tiled=...  120 us
    reduce_scatter x1, waiting for transfers between devices, body(): landed = lax.psum_scatter(shares, 'ctx', scatter_dimension=0, tiled=True)  114 us
    pallas_call x2, Pallas kernels, attention(): pl.pallas_call(functools.partial(attention_kernel, pair, tokens, part * r...  51.3 us
    reduce_scatter x1, waiting for transfers between devices, body(): landed = lax.psum_scatter(landed, 'head', scatter_dimension=1, tiled=True)  43.2 us
    all_gather x1, waiting for transfers between devices, body(): full_rows = lax.all_gather(joined, 'head', axis=1, tiled=True)  41.2 us
    reduce_scatter x2, waiting for transfers between devices, body(): lax.psum_scatter(partial_out.astype(jnp.bfloat16), 'head', scatter_dimens...  27.4 us
    all_gather x1, waiting for transfers between devices, body(): lax.all_gather(jnp.concatenate([keys, kv_rows[:, HD:]], 1).astype(jnp.bfl...  20.4 us
    pallas_call x1, Pallas kernels, spread_rows(): pl.pallas_call(functools.partial(spread_kernel, per_owner), grid=(blocks...  12.3 us
  transfers between devices with their start and end apart: 7, of which 6 were waited for; matrix products, arithmetic and copies ran while one was open for 3% of the time, Pallas kernels for 5%

commit v1 on v0

--- a/solution.py
+++ b/solution.py
@@ -34,27 +34,340 @@
     return jnp.einsum("rq,...qe->...re", lower, onehot, preferred_element_type=jnp.float32)
 
 
-def pick_kernel(pick_ref, rows_ref, out_ref):
-    for i in range(pick_ref.shape[0]):
-        out_ref[i] = jnp.dot(
-            pick_ref[i], rows_ref[i], preferred_element_type=jnp.float32
-        ).astype(out_ref.dtype)
-
-
-def pick_rows(pick, gathered, width):
-    blocks, capacity, rows = pick.shape
-    group = 4
+def split_ctx(ctx_count):
+    low = 2 if ctx_count % 2 == 0 else 1
+    middle = 2 if (ctx_count // low) % 2 == 0 else 1
+    return ctx_count // (low * middle), middle, low
+
+
+def choose(index, values):
+    result = values[0]
+    for i, value in enumerate(values[1:], 1):
+        result = jnp.where(index == i, value, result)
+    return result
+
+
+def expert_kernel(
+    ctx_count, heads, experts, rows, extra, capacity,
+    own_ref, gate_hbm, up_hbm,
+    gathered, hidden_ref,
+    gate_w, up_w, block_ref, inputs, scales, weight_sem, load_sem, own_sem, send_sem, recv_sem, half_sem,
+):
+    U, V, W = split_ctx(ctx_count)
+    ctx = lax.axis_index("ctx")
+    h = lax.axis_index("head")
+    u, v, w = ctx // (V * W), lax.rem(ctx // W, V), lax.rem(ctx, W)
+    width = own_ref.shape[1]
+    total = rows + extra
+    cut = (total // 2) // 16 * 16
+    mine = ctx * heads + h
+
+    def block_of(uu, vv, ww, hh):
+        return ((uu * V + vv) * W + ww) * heads + hh
+
+    def ctx_of(uu, vv, ww):
+        return (uu * V + vv) * W + ww
+
+    xs = [lax.rem(v + i, V) for i in range(1, V)]
+    ys = [lax.rem(u + i, U) for i in range(1, U)]
+    ws = [lax.rem(w + i, W) for i in range(1, W)]
+    lows = [h - s for s in range(heads)]
+    highs = [h + s for s in range(heads)]
+    peers = [({"ctx": ctx, "head": h - 1}, h > 0), ({"ctx": ctx, "head": h + 1}, h + 1 < heads)]
+    peers += [({"ctx": ctx_of(u, x, w), "head": h}, None) for x in xs]
+    peers += [({"ctx": ctx_of(y, v, w), "head": h}, None) for y in ys]
+    peers += [({"ctx": ctx_of(u, v, s), "head": h}, None) for s in ws]
+
+    def guarded(condition, action):
+        if condition is None:
+            action()
+        else:
+            pl.when(condition)(action)
+
+    def both(first, second):
+        if first is None:
+            return second
+        return first if second is None else first & second
+
+    def span(half):
+        if half is None:
+            return slice(None)
+        return pl.ds(0, cut) if half == 0 else pl.ds(cut, total - cut)
+
+    def recv_of(block, half):
+        return half_sem.at[block] if half == 1 else recv_sem.at[block]
+
+    sends = []
+
+    def plan(block, half, target, condition, own=False):
+        sends.append((block, half, target, condition, own))
+        return ("send", len(sends) - 1)
+
+    def copy_of(index):
+        block, half, target, condition, own = sends[index]
+        source = own_ref if own else gathered.at[block, span(half)]
+        return pltpu.make_async_remote_copy(
+            src_ref=source,
+            dst_ref=gathered.at[block, span(half)],
+            send_sem=send_sem.at[index],
+            recv_sem=recv_of(block, half),
+            device_id=target,
+            device_id_type=pl.DeviceIdType.MESH,
+        )
+
+    def wait_for(block, half, condition):
+        return ("wait", block, half, condition)
+
+    down = {"ctx": ctx, "head": h - 1}
+    upper = {"ctx": ctx, "head": h + 1}
+    across = [{"ctx": ctx_of(u, x, w), "head": h} for x in xs]
+    along = [{"ctx": ctx_of(y, v, w), "head": h} for y in ys]
+    partners = [{"ctx": ctx_of(u, v, s), "head": h} for s in ws]
+
+    def at_step(s):
+        if s == 0:
+            return [(h, None)]
+        return [(lows[s], lows[s] >= 0), (highs[s], highs[s] < heads)]
+
+    def column_step(s):
+        ops = []
+        for place, condition in at_step(s):
+            block = block_of(u, v, w, place)
+            own = s == 0
+            if not own:
+                ops.append(wait_for(block, None, condition))
+            if own or place is highs[s]:
+                ops.append(plan(block, None, down, both(condition, h > 0), own))
+            if own or place is lows[s]:
+                ops.append(plan(block, None, upper, both(condition, h + 1 < heads), own))
+            for target in across + along + partners:
+                ops.append(plan(block, None, target, condition, own))
+        return ops
+
+    def cross_step(s):
+        ops = []
+        for place, condition in at_step(s):
+            for x in xs:
+                block = block_of(u, x, w, place)
+                ops.append(wait_for(block, None, condition))
+                for target in along:
+                    ops.append(plan(block, 0, target, condition))
+                for target in partners:
+                    ops.append(plan(block, None, target, condition))
+            for y in ys:
+                block = block_of(y, v, w, place)
+                ops.append(wait_for(block, None, condition))
+                for target in across:
+                    ops.append(plan(block, 1, target, condition))
+                for target in partners:
+                    ops.append(plan(block, None, target, condition))
+        return ops
+
+    def corner_step(s):
+        ops = []
+        for place, condition in at_step(s):
+            for x in xs:
+                for y in ys:
+                    block = block_of(y, x, w, place)
+                    for half in (0, 1):
+                        ops.append(wait_for(block, half, condition))
+                        for target in partners:
+                            ops.append(plan(block, half, target, condition))
+        return ops
+
+    def foreign(uu, vv, halves):
+        ops = []
+        for s in ws:
+            for place in range(heads):
+                block = block_of(uu, vv, s, place)
+                ops += [wait_for(block, half, None) for half in halves]
+        return ops
+
+    stages = [[]]
+    groups = []
+    for s in range(heads):
+        stages[0] += column_step(s)
+        if s >= 1:
+            stages[0] += cross_step(s - 1)
+        if s >= 2:
+            stages[0] += corner_step(s - 2)
+    groups.append((u, v, w))
+    for s in ws:
+        stages.append(foreign(u, v, (None,)) if s is ws[0] else [])
+        groups.append((u, v, s))
+    last = cross_step(heads - 1)
+    if heads >= 2:
+        last += corner_step(heads - 2)
+    for x in xs:
+        stages.append(last)
+        last = []
+        groups.append((u, x, w))
+    for y in ys:
+        stages.append(last)
+        last = []
+        groups.append((y, v, w))
+    for s in ws:
+        for x in xs:
+            stages.append(foreign(u, x, (None,)) if s is ws[0] else [])
+            groups.append((u, x, s))
+        for y in ys:
+            stages.append(foreign(y, v, (None,)) if s is ws[0] else [])
+            groups.append((y, v, s))
+    first = True
+    for x in xs:
+        for y in ys:
+            stages.append(corner_step(heads - 1) if first else [])
+            first = False
+            groups.append((y, x, w))
+    for s in ws:
+        for x in xs:
+            for y in ys:
+                stages.append(foreign(y, x, (0, 1)) if s is ws[0] else [])
+                groups.append((y, x, s))
+    bases = [block_of(*place, 0) for place in groups]
+
+    def perform(ops):
+        for op in ops:
+            if op[0] == "send":
+                index = op[1]
+                guarded(sends[index][3], lambda index=index: copy_of(index).start())
+            else:
+                _, block, half, condition = op
+
+                def wait(block=block, half=half):
+                    pltpu.make_async_remote_copy(
+                        src_ref=gathered.at[block, span(half)],
+                        dst_ref=gathered.at[block, span(half)],
+                        send_sem=send_sem.at[0],
+                        recv_sem=recv_of(block, half),
+                        device_id={"ctx": ctx, "head": h},
+                        device_id_type=pl.DeviceIdType.MESH,
+                    ).wait_recv()
+
+                guarded(condition, wait)
+
+    gate_copy = pltpu.make_async_copy(gate_hbm, gate_w, weight_sem.at[0])
+    up_copy = pltpu.make_async_copy(up_hbm, up_w, weight_sem.at[1])
+    own_copy = pltpu.make_async_copy(own_ref, gathered.at[mine], own_sem)
+
+    barrier = pltpu.get_barrier_semaphore()
+    for target, condition in peers:
+        guarded(
+            condition,
+            lambda target=target: pl.semaphore_signal(
+                barrier, inc=1, device_id=target, device_id_type=pl.DeviceIdType.MESH
+            ),
+        )
+    count = len(peers) - 2 + (h > 0).astype(jnp.int32) + (h + 1 < heads).astype(jnp.int32)
+    pl.semaphore_wait(barrier, count)
+
+    slots = heads * capacity
+    chunks = width // 128
+    row_id = lax.broadcasted_iota(jnp.int32, (rows, rows), 0)
+    col_id = lax.broadcasted_iota(jnp.int32, (rows, rows), 1)
+    earlier = (row_id < col_id).astype(jnp.bfloat16)
+    slot_id = lax.broadcasted_iota(jnp.int32, (capacity, rows), 0)
+    note_id = lax.broadcasted_iota(jnp.int32, (extra, 128), 0)
+
+    def load(block, slot):
+        return pltpu.make_async_copy(gathered.at[block], block_ref.at[slot], load_sem.at[slot])
+
+    def note_row(slot, note):
+        tile = note // 8
+        place = pl.multiple_of(lax.rem(tile, chunks) * 128, 128)
+        line = (tile // chunks) * 8 + lax.rem(note, 8)
+        piece = block_ref[slot, pl.ds(rows, extra), pl.ds(place, 128)].astype(jnp.float32)
+        return jnp.sum(jnp.where(note_id == line, piece, 0.0), 0, keepdims=True)
+
+    def compute(base):
+        load(base, 0).start()
+
+        def each(i, carry):
+            slot = lax.rem(i, 2)
+            load(base + i, slot).wait()
+
+            @pl.when(i + 1 < heads)
+            def _():
+                load(base + i + 1, 1 - slot).start()
+
+            gate = note_row(slot, mine) + note_row(slot, experts + mine)
+            wanted = gate > 0.0
+            ones = jnp.broadcast_to(wanted.astype(jnp.float32), (16, rows)).astype(jnp.bfloat16)
+            rank = jnp.dot(ones, earlier, preferred_element_type=jnp.float32)[0:1].astype(jnp.int32)
+            pick = (slot_id == rank) & wanted
+            scale = jnp.sum(jnp.where(pick, gate, 0.0), 1, keepdims=True)
+            place = pl.multiple_of(i * capacity, 16)
+            inputs[pl.ds(place, capacity), :] = jnp.dot(
+                pick.astype(jnp.float32).astype(jnp.bfloat16),
+                block_ref[slot, pl.ds(0, rows), :],
+                preferred_element_type=jnp.float32,
+            ).astype(jnp.bfloat16)
+            scales[pl.ds(place, capacity), :] = jnp.broadcast_to(scale, (capacity, 128))
+            return carry
+
+        lax.fori_loop(0, heads, each, 0)
+        hidden_width = gate_w.shape[1]
+        step = 256 if hidden_width % 256 == 0 else hidden_width
+        given = inputs[...]
+        factor = scales[:, 0:1]
+        place = pl.ds(pl.multiple_of(base * capacity, 16), slots)
+        for n in range(0, hidden_width, step):
+            gate = jnp.dot(given, gate_w[:, n : n + step], preferred_element_type=jnp.float32)
+            up = jnp.dot(given, up_w[:, n : n + step], preferred_element_type=jnp.float32)
+            value = gate / (1.0 + jnp.exp(-gate)) * up * factor
+            hidden_ref[place, n : n + step] = value.astype(jnp.bfloat16)
+
+    own_copy.start()
+    gate_copy.start()
+    up_copy.start()
+    perform(stages[0])
+    own_copy.wait()
+    gate_copy.wait()
+    up_copy.wait()
+
+    def stage(t, carry):
+        for i in range(1, len(stages)):
+            if stages[i]:
+                pl.when(t == i)(functools.partial(perform, stages[i]))
+        compute(choose(t, bases))
+        return carry
+
+    lax.fori_loop(0, len(stages), stage, 0)
+    for index in range(len(sends)):
+        guarded(sends[index][3], lambda index=index: copy_of(index).wait_send())
+
+
+def expert_inputs(own, w_gate, w_up, ctx_count, heads, experts, rows, capacity):
+    devices = ctx_count * heads
+    total, width = own.shape
+    hidden_width = w_gate.shape[1]
     return pl.pallas_call(
-        pick_kernel,
-        grid=(blocks // group,),
-        in_specs=[
-            pl.BlockSpec((group, capacity, rows), lambda b: (b, 0, 0)),
-            pl.BlockSpec((group, rows, width), lambda b: (b, 0, 0)),
+        functools.partial(expert_kernel, ctx_count, heads, experts, rows, total - rows, capacity),
+        in_specs=[pl.BlockSpec(memory_space=pl.ANY)] * 3,
+        out_specs=[
+            pl.BlockSpec(memory_space=pl.ANY),
+            pl.BlockSpec(memory_space=pltpu.VMEM),
         ],
-        out_specs=pl.BlockSpec((group, capacity, width), lambda b: (b, 0, 0)),
-        out_shape=jax.ShapeDtypeStruct((blocks, capacity, width), jnp.bfloat16),
-        name="pick_rows",
-    )(pick, gathered)
+        out_shape=[
+            jax.ShapeDtypeStruct((devices, total, width), jnp.bfloat16),
+            jax.ShapeDtypeStruct((devices * capacity, hidden_width), jnp.bfloat16),
+        ],
+        scratch_shapes=[
+            pltpu.VMEM(w_gate.shape, jnp.bfloat16),
+            pltpu.VMEM(w_up.shape, jnp.bfloat16),
+            pltpu.VMEM((2, total, width), jnp.bfloat16),
+            pltpu.VMEM((heads * capacity, width), jnp.bfloat16),
+            pltpu.VMEM((heads * capacity, 128), jnp.float32),
+            pltpu.SemaphoreType.DMA((2,)),
+            pltpu.SemaphoreType.DMA((2,)),
+            pltpu.SemaphoreType.DMA,
+            pltpu.SemaphoreType.DMA((6 * devices,)),
+            pltpu.SemaphoreType.DMA((devices,)),
+            pltpu.SemaphoreType.DMA((devices,)),
+        ],
+        compiler_params=pltpu.CompilerParams(collective_id=0, has_side_effects=True),
+        name="expert_inputs",
+    )(own, w_gate, w_up)
 
 
 def spread_kernel(per_owner, pick_ref, rows_ref, out_ref):
@@ -223,50 +536,53 @@
     gates_low = gates - gates_high
     spots_high = (spots // 128).astype(jnp.float32)[:, None]
     spots_low = (spots % 128).astype(jnp.float32)[:, None]
-    extra = jnp.concatenate([gates_high, gates_low, spots_high, spots_low], 1).astype(jnp.bfloat16)
-    extra_width = -(-extra.shape[1] // 128) * 128
-    extra = jnp.pad(extra, ((0, 0), (0, extra_width - extra.shape[1])))
-    gathered = lax.all_gather(
-        jnp.concatenate([ordered, extra], 1), BOTH, axis=0, tiled=True
+    per_note = jnp.concatenate([gates_high, gates_low, spots_high, spots_low], 1).T
+    group_of = 8 * (model_width // 128)
+    note_groups = -(-per_note.shape[0] // group_of)
+    per_note = jnp.pad(per_note, ((0, note_groups * group_of - per_note.shape[0]), (0, 0)))
+    extra = (
+        per_note.reshape(note_groups, model_width // 128, 8, rows_here)
+        .transpose(0, 2, 1, 3)
+        .reshape(note_groups * 8, model_width)
+        .astype(jnp.bfloat16)
+    )
+    padded = -(-capacity // 16) * 16
+    gathered, hidden = expert_inputs(
+        jnp.concatenate([ordered, extra], 0),
+        w_gate[0], w_up[0], ctx_count, head_count, experts, rows_here, padded,
     )
 
     mine = ctx_here * head_count + head_here
-    notes = gathered[:, model_width:].astype(jnp.float32)
-    column = jnp.arange(extra_width, dtype=jnp.int32)
+    notes = (
+        gathered[:, rows_here:]
+        .reshape(devices, note_groups, 8, model_width // 128, rows_here)
+        .transpose(0, 1, 3, 2, 4)
+        .reshape(devices, note_groups * group_of, rows_here)
+        .astype(jnp.float32)
+    )
+    note_ids = jnp.arange(note_groups * group_of, dtype=jnp.int32)[:, None]
     my_gate = jnp.sum(
-        jnp.where((column == mine) | (column == experts + mine), notes, 0.0), 1
-    ).reshape(devices, rows_here)
+        jnp.where((note_ids == mine) | (note_ids == experts + mine), notes, 0.0), 1
+    )
     wanted = my_gate > 0.0
     rank = exclusive_count(wanted.astype(jnp.bfloat16)[:, :, None])[:, :, 0].astype(jnp.int32)
-    pick = (
-        (rank[:, None, :] == jnp.arange(capacity, dtype=jnp.int32)[None, :, None])
-        & wanted[:, None, :]
-    )
-    slot_gate = jnp.sum(jnp.where(pick, my_gate[:, None, :], 0.0), -1)
-    pick_bf = pick.astype(jnp.bfloat16)
     back_bf = (
-        (rank[:, :, None] == jnp.arange(capacity, dtype=jnp.int32)[None, None, :])
+        (rank[:, :, None] == jnp.arange(padded, dtype=jnp.int32)[None, None, :])
         & wanted[:, :, None]
     ).astype(jnp.bfloat16)
-    inputs = pick_rows(
-        pick_bf, gathered.reshape(devices, rows_here, -1), model_width
-    ).reshape(devices * capacity, model_width)
-    gate_part = jnp.dot(inputs, w_gate[0], preferred_element_type=jnp.float32)
-    upward = jnp.dot(inputs, w_up[0], preferred_element_type=jnp.float32)
-    hidden = (jax.nn.silu(gate_part) * upward).astype(jnp.bfloat16)
-    produced = jnp.dot(hidden, w_down[0], preferred_element_type=jnp.float32)
-    weighted = (produced * slot_gate.reshape(-1, 1)).astype(jnp.bfloat16)
+    weighted = jnp.dot(hidden, w_down[0], preferred_element_type=jnp.float32).astype(jnp.bfloat16)
     shares = spread_rows(
-        back_bf, weighted.reshape(devices, capacity, model_width), ctx_count
+        back_bf, weighted.reshape(devices, padded, model_width), ctx_count
     ).reshape(devices * rows_here, model_width)
     landed = lax.psum_scatter(shares, "ctx", scatter_dimension=0, tiled=True)
     landed = lax.psum_scatter(landed, "head", scatter_dimension=1, tiled=True)
 
-    notes4 = notes.reshape(devices, ctx_count, per_owner, extra_width)
-    notes_here = lax.dynamic_index_in_dim(notes4, ctx_here, 1, keepdims=False)
+    spots_all = (notes[:, 2 * experts] * 128.0 + notes[:, 2 * experts + 1]).reshape(
+        devices, ctx_count, per_owner
+    )
     spot_ids = (
-        notes_here[:, :, 2 * experts] * 128.0 + notes_here[:, :, 2 * experts + 1]
-    ).astype(jnp.int32).reshape(-1)
+        lax.dynamic_index_in_dim(spots_all, ctx_here, 1, keepdims=False).astype(jnp.int32).reshape(-1)
+    )
     aimed = (
         jnp.arange(local_tokens, dtype=jnp.int32)[:, None] == spot_ids[None, :]
     ).astype(jnp.bfloat16)

time: 526 us -> 506 us (0.962)
  waiting for transfers between devices: 366 us -> 258 us
  Pallas kernels: 75.2 us -> 174 us
  matrix products: 44.3 us -> 32.1 us
    all_gather x1 -> x0, waiting for transfers between devices: 120 us -> none  [body(): lax.all_gather(jnp.concatenate([ordered, extra], 1), BOTH, axis=0, tiled=...]
    pallas_call x1, Pallas kernels: 11.6 us -> 110 us  [expert_inputs(): pl.pallas_call(functools.partial(expert_kernel, ctx_count, heads, experts...]
    reduce_scatter x1, waiting for transfers between devices: 114 us -> 130 us  [body(): landed = lax.psum_scatter(shares, 'ctx', scatter_dimension=0, tiled=True)]
    dot_general x3 -> x1, matrix products: 20.9 us -> 8.67 us  [body(): jnp.dot(hidden, w_down[0], preferred_element_type=jnp.float32)]
  transfers between devices with their start and end apart: 7 -> 6, of which waited for: 6 -> 5; matrix products, arithmetic and copies ran while one was open for 3% -> 4% of each run, Pallas kernels for 5% -> 5%
where the time goes in v1:
time: 506 us; the launch traced here: 502 us
  waiting for transfers between devices  258 us (51%)
  Pallas kernels  174 us (34%)
  matrix products  32.1 us (6%)
  other arithmetic  16.4 us (3%)
  between operations  13.7 us (3%)
  local copies, waits for them, and re-layouts  7.07 us (1%)
    reduce_scatter x1, waiting for transfers between devices, body(): landed = lax.psum_scatter(shares, 'ctx', scatter_dimension=0, tiled=True)  130 us
    pallas_call x1, Pallas kernels, expert_inputs(): pl.pallas_call(functools.partial(expert_kernel, ctx_count, heads, experts...  110 us
    pallas_call x2, Pallas kernels, attention(): pl.pallas_call(functools.partial(attention_kernel, pair, tokens, part * r...  51.3 us
    all_gather x1, waiting for transfers between devices, body(): full_rows = lax.all_gather(joined, 'head', axis=1, tiled=True)  41.3 us
    reduce_scatter x1, waiting for transfers between devices, body(): landed = lax.psum_scatter(landed, 'head', scatter_dimension=1, tiled=True)  39.4 us
    reduce_scatter x2, waiting for transfers between devices, body(): lax.psum_scatter(partial_out.astype(jnp.bfloat16), 'head', scatter_dimens...  27.4 us
    all_gather x1, waiting for transfers between devices, body(): lax.all_gather(jnp.concatenate([keys, kv_rows[:, HD:]], 1).astype(jnp.bfl...  20.3 us
    pallas_call x1, Pallas kernels, spread_rows(): pl.pallas_call(functools.partial(spread_kernel, per_owner), grid=(blocks...  12.3 us
  transfers between devices with their start and end apart: 6, of which 5 were waited for; matrix products, arithmetic and copies ran while one was open for 4% of the time, Pallas kernels for 5%

profile of v1, /device:TPU:7, one launch (start us, length us, event | category | flops | bytes accessed | tf_op | source)
XLA Modules:
  0.0 501.6 jit_solution(11179495898039785546)
XLA Ops:
  6.6 0.8 and_select_fusion.3
  7.4 0.1 fusion.7
  7.5 0.1 select_reduce_fusion.1
  7.7 0.8 convolution_convert_fusion.5
  8.5 1.3 convolution_convert_fusion.3
  9.9 1.2 select_reduce_fusion.2
  11.2 0.9 pad_maximum_fusion.own_ref
  12.0 110.1 %expert_inputs.1 = (bf16[32,136,2048]{2,1,0:T(8,128)(2,1)}, bf16[1536,768]{1,0:T(8,128)(2,1)}) custom-call(bf16[136,2048]{1,0:T(8,128)(2,1)} %pad_maximum_fusion.own_ref, bf16[2048,768]{1,0:T(8,128)(2,1)} %bitcast.60, bf16[2048,768]{1,0:T(8,128)(2,1)} %bitcast.61), custom_call_target="tpu_custom_call" | custom-call | tf_op jit(solution)/shard_map/expert_inputs/pallas_call | solution.py:344
  122.1 1.5 select_reduce_fusion
  123.7 0.1 convolution_convert_fusion.4
  123.8 2.4 fusion.5.pick_ref
  126.2 8.7 %convolution_convert_fusion = bf16[1536,2048]{1,0:T(8,128)(2,1)} fusion(bf16[1536,768]{1,0:T(8,128)(2,1)} %get-tuple-element.8, bf16[1,768,2048]{2,1,0:T(8,128)(2,1)S(1)} %copy-done), kind=kOutput, calls=%fused_computation | convolution fusion | flops 4834983936 | bytes 11796480 | tf_op jit(solution)/shard_map/dot_general | solution.py:573
  134.9 12.3 %spread_rows.1 = bf16[8,32,16,2048]{3,2,1,0:T(8,128)(2,1)} custom-call(bf16[32,128,48]{2,1,0:T(8,128)(2,1)} %fusion.5.pick_ref, bf16[32,48,2048]{2,1,0:T(8,128)(2,1)} %bitcast.59), custom_call_target="tpu_custom_call" | custom-call | tf_op jit(solution)/shard_map/spread_rows/pallas_call | solution.py:386
  147.2 0.0 reduce-scatter.7.cloned.1.call-start
  147.3 129.8 %reduce-scatter.5.cloned.1.call-done = bf16[512,2048]{1,0:T(8,128)(2,1)} async-done(((bf16[4096,2048]{1,0:T(8,128)(2,1)}), bf16[512,2048]{1,0:T(8,128)(2,1)}) %reduce-scatter.5.cloned.1.call-update) | async-done | bytes 2097168 | tf_op jit(solution)/shard_map/reduce_scatter | solution.py:577
  277.1 0.0 reduce-scatter.7.cloned.1.call-update
  277.1 0.0 all-gather.3.cloned.1.call-start
  277.1 1.5 convert_bitcast_fusion
  278.6 4.7 copy.24
  283.3 0.9 slice_add_fusion
  284.2 0.1 copy.25
  284.3 0.1 convert_element_type.142
  284.4 39.4 %reduce-scatter.7.cloned.1.call-done = bf16[512,512]{1,0:T(8,128)(2,1)} async-done(((bf16[512,2048]{1,0:T(8,128)(2,1)}), bf16[512,512]{1,0:T(8,128)(2,1)}) %reduce-scatter.7.cloned.1.call-update) | async-done | bytes 524304 | tf_op jit(solution)/shard_map/reduce_scatter | solution.py:578
  323.8 2.3 fusion.6
  326.1 0.0 all-gather.5.cloned.1.call-start
  326.2 0.8 dynamic_slice.16
  327.0 1.8 fusion.19
  328.7 1.3 constant_dynamic-slice_fusion
  330.0 41.3 %all-gather.3.cloned.1.call-done = bf16[512,2048]{1,0:T(8,128)(2,1)} async-done(((bf16[512,512]{1,0:T(8,128)(2,1)}), bf16[512,2048]{1,0:T(8,128)(2,1)}) %all-gather.3.cloned.1.call-update) | async-done | bytes 2097168 | tf_op jit(solution)/shard_map/all_gather | solution.py:592
  371.3 2.1 fusion
  373.4 2.4 fusion.8
  375.8 0.1 multiply_reduce_fusion
  376.0 0.1 multiply_multiply_fusion
  376.2 0.1 fusion.33
  376.3 1.1 fusion.17
  377.5 0.7 pad_maximum_fusion.4
  378.2 0.0 all-gather.5.cloned.1.call-update
  378.2 0.2 reduce-scatter.9.cloned.1.call-start
  378.5 5.9 %fusion.13.q_ref = f32[512,1024]{1,0:T(8,128)} fusion(bf16[2048,1024]{1,0:T(8,128)(2,1)} %param.26, bf16[512,2048]{1,0:T(8,128)(2,1)S(1)} %copy-done.2, f32[2048]{0:T(1024)S(1)} %copy-done.5, f32[512]{0:T(512)S(1)} %add_rsqrt_fusion.1), kind=kOutput, calls=%fused_computation.26 | convolution fusion | flops 2151677952 | bytes 8398848 | tf_op jit(solution)/shard_map/dot_general | solution.py:618
  384.3 20.3 %all-gather.5.cloned.1.call-done.kv_ref = bf16[4096,256]{1,0:T(8,128)(2,1)} async-done(((bf16[512,256]{1,0:T(8,128)(2,1)}), bf16[4096,256]{1,0:T(8,128)(2,1)}) %all-gather.5.cloned.1.call-update) | async-done | bytes 2097168 | tf_op jit(solution)/shard_map/all_gather | solution.py:615
  404.6 26.1 %attention_0.1 = bf16[256,1024]{1,0:T(8,128)(2,1)} custom-call(f32[512,1024]{1,0:T(8,128)} %fusion.13.q_ref, f32[512,128]{1,0:T(8,128)} %get-tuple-element.13.cos_ref, f32[512,128]{1,0:T(8,128)} %get-tuple-element.10.sin_ref, f32[1,1024]{1,0:T(1,128)} %bitcast.63, bf16[4096,256]{1,0:T(8,128)(2,1)} %all-gather.5.cloned.1.call-done.kv_ref), custom_call_target="tpu_custom_call" | custom-call | flops 8589934592 | bytes 2097152 | tf_op jit(solution)/shard_map/attention_0/pallas_call | solution.py:462
  430.7 4.6 convolution_convert_fusion.2
  435.3 0.0 reduce-scatter.11.cloned.1.call-start
  435.3 25.2 %attention_1.1 = bf16[256,1024]{1,0:T(8,128)(2,1)} custom-call(f32[512,1024]{1,0:T(8,128)} %fusion.13.q_ref, f32[512,128]{1,0:T(8,128)} %get-tuple-element.13.cos_ref, f32[512,128]{1,0:T(8,128)} %get-tuple-element.10.sin_ref, f32[1,1024]{1,0:T(1,128)} %bitcast.64, bf16[4096,256]{1,0:T(8,128)(2,1)} %all-gather.5.cloned.1.call-done.kv_ref), custom_call_target="tpu_custom_call" | custom-call | flops 8589934592 | bytes 2097152 | tf_op jit(solution)/shard_map/attention_1/pallas_call | solution.py:462
  460.5 4.6 convolution_convert_fusion.1
  465.2 0.0 reduce-scatter.9.cloned.1.call-done
  465.2 27.4 %reduce-scatter.11.cloned.1.call-done = bf16[256,512]{1,0:T(8,128)(2,1)} async-done(((bf16[256,2048]{1,0:T(8,128)(2,1)}), bf16[256,512]{1,0:T(8,128)(2,1)}) %reduce-scatter.11.cloned.1.call-update) | async-done | bytes 262160 | tf_op jit(solution)/shard_map/reduce_scatter | solution.py:625
  492.6 2.1 add_convert_fusion.1
  (33 shorter events, 0.3 us)
Async XLA Ops:
  6.5 119.7 %copy-start = (bf16[1,768,2048]{2,1,0:T(8,128)(2,1)S(1)}, bf16[1,768,2048]{2,1,0:T(8,128)(2,1)}, u32[]{:S(2)}) copy-start(bf16[1,768,2048]{2,1,0:T(8,128)(2,1)} %param.21) | copy-start | bytes 9437188
  6.5 270.5 %reduce-scatter.5.cloned.1.call-start = ((), (), s32[]{:S(2)}) async-start(), calls=%async_computation.4 | async-start | bytes 18874368 | tf_op jit(solution)/shard_map/reduce_scatter | solution.py:577
  147.2 176.6 %reduce-scatter.7.cloned.1.call-start = ((), (), s32[]{:S(2)}) async-start(), calls=%async_computation.5 | async-start | bytes 2621440 | tf_op jit(solution)/shard_map/reduce_scatter | solution.py:578
  277.1 94.2 %all-gather.3.cloned.1.call-start = ((), (), s32[]{:S(2)}) async-start(), calls=%async_computation.6 | async-start | bytes 2621440 | tf_op jit(solution)/shard_map/all_gather | solution.py:592
  278.6 45.2 %copy-start.4 = (bf16[512,512]{1,0:T(8,128)(2,1)S(1)}, bf16[512,512]{1,0:T(8,128)(2,1)}, u32[]{:S(2)}) copy-start(bf16[512,512]{1,0:T(8,128)(2,1)} %param.22) | copy-start | bytes 1572868
  326.1 47.3 %copy-start.5 = (f32[2048]{0:T(1024)S(1)}, f32[2048]{0:T(1024)}, u32[]{:S(2)}) copy-start(f32[2048]{0:T(1024)} %param.23) | copy-start | bytes 24580
  326.1 78.5 %all-gather.5.cloned.1.call-start = ((), (), s32[]{:S(2)}) async-start(), calls=%async_computation.7 | async-start | bytes 2359296 | tf_op jit(solution)/shard_map/all_gather | solution.py:615
  373.4 2.9 copy-start.3
  375.8 2.6 copy-start.2
  378.2 87.0 %reduce-scatter.9.cloned.1.call-start = ((), (), s32[]{:S(2)}) async-start(), calls=%async_computation.8 | async-start | bytes 1310720 | tf_op jit(solution)/shard_map/reduce_scatter | solution.py:625
  435.3 57.3 %reduce-scatter.11.cloned.1.call-start = ((), (), s32[]{:S(2)}) async-start(), calls=%async_computation.9 | async-start | bytes 1310720 | tf_op jit(solution)/shard_map/reduce_scatter | solution.py:625
  435.3 59.4 %copy-start.1 = (bf16[1,768,2048]{2,1,0:T(8,128)(2,1)S(1)}, bf16[1,768,2048]{2,1,0:T(8,128)(2,1)}, u32[]{:S(2)}) copy-start(bf16[1,768,2048]{2,1,0:T(8,128)(2,1)} %param.21) | copy-start | bytes 9437188
Sparse Core Ops, SparseCore 0:
  147.4 129.6 reduce-scatter.4
  279.4 44.4 reduce-scatter.6
  326.3 45.0 all-gather.2
  378.3 26.2 all-gather.4
  435.4 26.9 reduce-scatter.8
  465.3 27.2 reduce-scatter.10
